TPU v7x, 512 devices: a whole 4x4x16 slice. The times are simulated.
512 devices in a mesh: seq: 64 (over z, y), tp: 8 (over x, core).
Axes of the slice: x: 4, y: 4, z: 16, core: 2. Of those that a mesh axis runs over, the one named last changes fastest.
Arguments:
- query_proj: bfloat16 [4096, 8192], P('tp', 'seq'), may hold values from -6 to 6
- key_proj: bfloat16 [4096, 8192], P('tp', 'seq'), may hold values from -6 to 6
- value_proj: bfloat16 [4096, 8192], P('tp', 'seq'), may hold values from -6 to 6
- short_taps: float32 [3, 3, 4096], P(None, None, 'tp'), may hold values from -3.5 to 3.5
- long_filters: float32 [4096, 8192], P(('tp', 'seq')), may hold values from -2 to 2
- out_weight: bfloat16 [4096, 8192], P('seq', 'tp'), may hold values from -0.09375 to 0.09375
Outputs:
- block_out: bfloat16 [8192, 8192], P('seq', 'tp')
All inputs are finite; a program needn't handle non-finite values.
Results may differ from a plain program's by a relative error of at most 0.0058.
Values may be sent and summed in bfloat16 or wider, within the bound.
A program may use at most 64 MiB of HBM per device.

v0:
```python
import math
import jax
import jax.numpy as jnp
from jax import lax
from jax.sharding import PartitionSpec as P

precise = lax.Precision.HIGHEST


def shifted(value, axis, steps):
    count = lax.axis_size(axis)
    initial, last = (max(0, -steps), min(count, count - steps))
    return lax.ppermute(value, axis, [(source, source + steps) for source in range(initial, last)])


def short_filter(extended, tap_weights):
    return (
        tap_weights[0][:, None] * extended[:, 2:]
        + tap_weights[1][:, None] * extended[:, 1:-1]
        + tap_weights[2][:, None] * extended[:, :-2]
    )


def phase_table(period, out_size, in_size, direction):
    out_index = lax.broadcasted_iota(jnp.int32, (out_size, in_size), 0)
    in_index = lax.broadcasted_iota(jnp.int32, (out_size, in_size), 1)
    phase_angle = (out_index * in_index % period).astype(jnp.float32) * (
        direction * 2.0 * math.pi / period
    )
    return (jnp.cos(phase_angle), jnp.sin(phase_angle))


def left_apply(phase, signal):
    return jnp.einsum("kn,cnm->ckm", phase, signal, precision=precise)


def right_apply(signal, phase):
    return jnp.einsum("ckn,nm->ckm", signal, phase, precision=precise)


def forward_spectrum(signal, inner_size):
    channels_here, length = signal.shape
    period = 2 * length
    outer_size = period // inner_size
    blocks = signal.reshape(channels_here, outer_size // 2, inner_size)
    left_re, left_im = phase_table(outer_size, outer_size, outer_size // 2, -1.0)
    section_re = left_apply(left_re, blocks)
    section_im = left_apply(left_im, blocks)
    twist_re, twist_im = phase_table(period, outer_size, inner_size, -1.0)
    turned_re = section_re * twist_re - section_im * twist_im
    turned_im = section_re * twist_im + section_im * twist_re
    right_re, right_im = phase_table(inner_size, inner_size, inner_size, -1.0)
    spec_re = right_apply(turned_re, right_re) - right_apply(turned_im, right_im)
    spec_im = right_apply(turned_re, right_im) + right_apply(turned_im, right_re)
    return (spec_re, spec_im)


def inverse_signal(spec_re, spec_im, length, inner_size):
    channels_here = spec_re.shape[0]
    period = 2 * length
    outer_size = period // inner_size
    right_re, right_im = phase_table(inner_size, inner_size, inner_size, 1.0)
    mid_re = right_apply(spec_re, right_re) - right_apply(spec_im, right_im)
    mid_im = right_apply(spec_re, right_im) + right_apply(spec_im, right_re)
    twist_re, twist_im = phase_table(period, outer_size, inner_size, 1.0)
    turned_re = mid_re * twist_re - mid_im * twist_im
    turned_im = mid_re * twist_im + mid_im * twist_re
    left_re, left_im = phase_table(outer_size, outer_size // 2, outer_size, 1.0)
    signal = left_apply(left_re, turned_re) - left_apply(left_im, turned_im)
    return signal.reshape(channels_here, length) / period


def long_convolve(signal, filters, inner_size):
    length = signal.shape[1]
    data_re, data_im = forward_spectrum(signal, inner_size)
    filt_re, filt_im = forward_spectrum(filters, inner_size)
    prod_re = data_re * filt_re - data_im * filt_im
    prod_im = data_re * filt_im + data_im * filt_re
    return inverse_signal(prod_re, prod_im, length, inner_size)


def shards(query_proj, key_proj, value_proj, short_taps, long_filters, out_weight):
    tok_rows = query_proj.shape[1]
    inner_size = tok_rows // 2
    tail_cols = jnp.stack([query_proj[:, -2:], key_proj[:, -2:], value_proj[:, -2:]])
    before = shifted(tail_cols, "seq", 1)
    shorts = []
    for stream_index, stream in enumerate((query_proj, key_proj, value_proj)):
        extended = jnp.concatenate([before[stream_index], stream], axis=1).astype(jnp.float32)
        shorts.append(short_filter(extended, short_taps[stream_index]))
    query_short, key_short, value_short = shorts
    product = (key_short * value_short).astype(jnp.bfloat16)
    spread = lax.all_to_all(product, "seq", split_axis=0, concat_axis=1, tiled=True)
    mixed_conv = long_convolve(spread.astype(jnp.float32), long_filters, inner_size)
    returned = lax.all_to_all(mixed_conv, "seq", split_axis=1, concat_axis=0, tiled=True)
    gated_out = (query_short * returned).astype(jnp.bfloat16)
    full_rows = lax.all_gather(gated_out, "tp", axis=0, tiled=True)
    result = lax.dot_general(
        full_rows,
        lax.all_gather(out_weight, "seq", axis=0, tiled=True),
        (((0,), (0,)), ((), ())),
        preferred_element_type=jnp.float32,
    )
    return result.astype(jnp.bfloat16)


def solution(mesh):
    return jax.shard_map(
        shards,
        mesh=mesh,
        in_specs=(
            P("tp", "seq"),
            P("tp", "seq"),
            P("tp", "seq"),
            P(None, None, "tp"),
            P(("tp", "seq"), None),
            P("seq", "tp"),
        ),
        out_specs=P("seq", "tp"),
        check_vma=False,
    )
```

profile of v0, /device:TPU:2, one launch (start us, length us, event | category | flops | bytes accessed | tf_op | source)
XLA Modules:
  0.0 292.9 jit_solution(1270531788461723805)
XLA Ops:
  6.5 1.0 slice.94
  7.7 1.0 slice.95
  8.8 1.0 slice.96
  10.3 3.5 %collective-permute-start = (bf16[3,512,2]{2,1,0:T(8,128)(2,1)S(1)}, bf16[3,512,2]{2,1,0:T(8,128)(2,1)S(1)}, u32[]{:S(2)}, u32[]{:S(2)}) collective-permute-start(bf16[3,512,2]{2,1,0:T(8,128)(2,1)S(1)} %copy.25), channel_id=1, source_target_pairs={{0,8},{8,16},{16,24},{24,32},{32,40},{40,48},{48,56},{56,64},{64,7... | collective-permute-start | bytes 18440 | tf_op jit(solution)/shard_map/ppermute | solution.py:13
  14.1 1.1 reshape.82
  15.4 1.1 fusion.58
  16.5 1.1 fusion.61
  17.6 0.9 fusion.180
  18.4 0.8 fusion.4
  19.2 0.8 convolution_add_fusion.1
  20.3 1.8 collective-permute-done
  22.4 1.4 fusion.47
  23.8 20.5 %all-to-all-start = ((bf16[64,8,128]{2,1,0:T(8,128)(2,1)}), bf16[64,8,128]{2,1,0:T(8,128)(2,1)S(1)}, u32[]{:S(2)}, u32[]{:S(2)}) async-start(bf16[64,8,128]{2,1,0:T(8,128)(2,1)} %fusion.47), calls=%async_computation | async-start | bytes 262144 | tf_op jit(solution)/shard_map/all_to_all | solution.py:93
  44.3 0.8 fusion.6
  45.1 0.8 convolution_subtract_fusion.1
  45.9 15.1 %all-to-all-done = bf16[64,8,128]{2,1,0:T(8,128)(2,1)S(1)} async-done(((bf16[64,8,128]{2,1,0:T(8,128)(2,1)}), bf16[64,8,128]{2,1,0:T(8,128)(2,1)S(1)}, u32[]{:S(2)}, u32[]{:S(2)}) %all-to-all-start) | async-done | bytes 131104 | tf_op jit(solution)/shard_map/all_to_all | solution.py:93
  61.1 0.9 convolution_bitcast_fusion
  62.0 0.9 convolution_bitcast_fusion.1
  62.9 0.8 fusion.48
  63.7 0.8 fusion.49
  64.5 0.8 convolution_subtract_fusion.2
  65.3 0.9 multiply_add_fusion
  67.0 0.7 fusion.67
  69.2 1.1 fusion.11
  70.3 1.1 fusion.1
  71.7 1.1 copy.32
  72.8 4.6 %all-to-all-start.1 = ((f32[8,64,128]{2,0,1:T(8,128)}), f32[8,64,128]{2,0,1:T(8,128)S(1)}, u32[]{:S(2)}, u32[]{:S(2)}) async-start(f32[8,64,128]{2,0,1:T(8,128)} %copy.32), calls=%async_computation.1 | async-start | bytes 524288 | tf_op jit(solution)/shard_map/all_to_all | solution.py:95
  77.6 21.1 %all-to-all-done.1 = f32[8,64,128]{2,0,1:T(8,128)S(1)} async-done(((f32[8,64,128]{2,0,1:T(8,128)}), f32[8,64,128]{2,0,1:T(8,128)S(1)}, u32[]{:S(2)}, u32[]{:S(2)}) %all-to-all-start.1) | async-done | bytes 262176 | tf_op jit(solution)/shard_map/all_to_all | solution.py:95
  98.8 1.1 fusion.23
  100.6 19.3 %all-gather.3.cloned.1.call-done = bf16[4096,128]{1,0:T(8,128)(2,1)} async-done(((bf16[512,128]{1,0:T(8,128)(2,1)}), bf16[4096,128]{1,0:T(8,128)(2,1)}) %all-gather.3.cloned.1.call-update) | async-done | bytes 1048592 | tf_op jit(solution)/shard_map/all_gather | solution.py:97
  120.0 160.3 %all-gather.5.cloned.1.call-done = bf16[4096,1024]{1,0:T(8,128)(2,1)} async-done(((bf16[64,1024]{1,0:T(8,128)(2,1)}), bf16[4096,1024]{1,0:T(8,128)(2,1)}) %all-gather.5.cloned.1.call-update) | async-done | bytes 8388624 | tf_op jit(solution)/shard_map/all_gather | solution.py:100
  280.3 5.7 %convolution_convert_fusion = bf16[128,1024]{1,0:T(8,128)(2,1)} fusion(bf16[4096,128]{1,0:T(8,128)(2,1)} %all-gather.3.cloned.1.call-done, bf16[4096,1024]{1,0:T(8,128)(2,1)} %all-gather.5.cloned.1.call-done), kind=kOutput, calls=%fused_computation.8 | convolution fusion | flops 1073872896 | bytes 9699328 | tf_op jit(solution)/shard_map/dot_general | solution.py:98
  (28 shorter events, 5.2 us)
Async XLA Ops:
  6.5 15.6 %copy-start.1 = (bf16[512,128]{1,0:T(8,128)(2,1)S(1)}, bf16[512,128]{1,0:T(8,128)(2,1)}, u32[]{:S(2)}) copy-start(bf16[512,128]{1,0:T(8,128)(2,1)} %param.7) | copy-start | bytes 393220
  6.5 15.6 %copy-start = (bf16[512,128]{1,0:T(8,128)(2,1)S(1)}, bf16[512,128]{1,0:T(8,128)(2,1)}, u32[]{:S(2)}) copy-start(bf16[512,128]{1,0:T(8,128)(2,1)} %param.8) | copy-start | bytes 393220
  10.3 11.8 %collective-permute-start = (bf16[3,512,2]{2,1,0:T(8,128)(2,1)S(1)}, bf16[3,512,2]{2,1,0:T(8,128)(2,1)S(1)}, u32[]{:S(2)}, u32[]{:S(2)}) collective-permute-start(bf16[3,512,2]{2,1,0:T(8,128)(2,1)S(1)} %copy.25), channel_id=1, source_target_pairs={{0,8},{8,16},{16,24},{24,32},{32,40},{40,48},{48,56},{56,64},{64,7... | collective-permute-start | bytes 18440 | tf_op jit(solution)/shard_map/ppermute | solution.py:13
  23.8 37.2 %all-to-all-start = ((bf16[64,8,128]{2,1,0:T(8,128)(2,1)}), bf16[64,8,128]{2,1,0:T(8,128)(2,1)S(1)}, u32[]{:S(2)}, u32[]{:S(2)}) async-start(bf16[64,8,128]{2,1,0:T(8,128)(2,1)} %fusion.47), calls=%async_computation | async-start | bytes 262144 | tf_op jit(solution)/shard_map/all_to_all | solution.py:93
  64.5 13.0 %copy-start.2 = (bf16[512,128]{1,0:T(8,128)(2,1)S(1)}, bf16[512,128]{1,0:T(8,128)(2,1)}, u32[]{:S(2)}) copy-start(bf16[512,128]{1,0:T(8,128)(2,1)} %param.6) | copy-start | bytes 393220
  72.8 26.0 %all-to-all-start.1 = ((f32[8,64,128]{2,0,1:T(8,128)}), f32[8,64,128]{2,0,1:T(8,128)S(1)}, u32[]{:S(2)}, u32[]{:S(2)}) async-start(f32[8,64,128]{2,0,1:T(8,128)} %copy.32), calls=%async_computation.1 | async-start | bytes 524288 | tf_op jit(solution)/shard_map/all_to_all | solution.py:95
  77.4 42.5 %all-gather.3.cloned.1.call-start = ((), (), s32[]{:S(2)}) async-start(), calls=%async_computation.2 | async-start | bytes 1179648 | tf_op jit(solution)/shard_map/all_gather | solution.py:97
  99.9 180.4 %all-gather.5.cloned.1.call-start = ((), (), s32[]{:S(2)}) async-start(), calls=%async_computation.3 | async-start | bytes 8519680 | tf_op jit(solution)/shard_map/all_gather | solution.py:100
Sparse Core Ops, SparseCore 0:
  100.0 19.9 all-gather.2
  122.9 157.3 all-gather.4
where the time goes:
time: 293 us
  waiting for transfers between devices  218 us (74%)
  starting transfers between devices  28.7 us (10%)
  matrix products  21.1 us (7%)
  between operations  13.7 us (5%)
  local copies, waits for them, and re-layouts  7.47 us (3%)
  other arithmetic  3.41 us (1%)
    all_gather x1, waiting for transfers between devices, shards(): lax.all_gather(out_weight, 'seq', axis=0, tiled=True)  160 us
    all_to_all x1, waiting for transfers between devices, shards(): lax.all_to_all(mixed_conv, 'seq', split_axis=1, concat_axis=0, tiled=True)  21.1 us
    all_to_all x1, starting transfers between devices, shards(): lax.all_to_all(product, 'seq', split_axis=0, concat_axis=1, tiled=True)  20.5 us
    all_gather x1, waiting for transfers between devices, shards(): full_rows = lax.all_gather(gated_out, 'tp', axis=0, tiled=True)  19.3 us
    all_to_all x1, waiting for transfers between devices, shards(): lax.all_to_all(product, 'seq', split_axis=0, concat_axis=1, tiled=True)  15.1 us
    dot_general x12, matrix products, right_apply(): return jnp.einsum('ckn,nm->ckm', signal, phase, precision=precise)  9.29 us
  transfers between devices with their start and end apart: 5, of which 5 were waited for; matrix products, arithmetic and copies ran while one was open for 3% of the time, Pallas kernels for 0%

commit v1 on v0

--- a/solution.py
+++ b/solution.py
@@ -94,7 +94,9 @@
     mixed_conv = long_convolve(spread.astype(jnp.float32), long_filters, inner_size)
     returned = lax.all_to_all(mixed_conv, "seq", split_axis=1, concat_axis=0, tiled=True)
     gated_out = (query_short * returned).astype(jnp.bfloat16)
-    full_rows = lax.all_gather(gated_out, "tp", axis=0, tiled=True)
+    full_rows = jnp.concatenate(
+        lax.all_to_all(jnp.stack([gated_out] * lax.axis_size("tp")), "tp", 0, 0), axis=0
+    )
     result = lax.dot_general(
         full_rows,
         lax.all_gather(out_weight, "seq", axis=0, tiled=True),

time: 293 us -> 186 us (0.63)
  waiting for transfers between devices: 218 us -> 92.7 us
  blocking collectives: 0 us -> 19.5 us
    all_gather x1, waiting for transfers between devices: 160 us -> 52.6 us  [shards(): lax.all_gather(out_weight, 'seq', axis=0, tiled=True)]
    all_to_all x0 -> x1, blocking collectives: none -> 19.5 us  [shards(): lax.all_to_all(jnp.stack([gated_out] * lax.axis_size('tp')), 'tp', 0, 0)]
    all_gather x1 -> x0, waiting for transfers between devices: 19.3 us -> none  [shards(): full_rows = lax.all_gather(gated_out, 'tp', axis=0, tiled=True)]
  transfers between devices with their start and end apart: 5 -> 4, of which waited for: 5 -> 4; matrix products, arithmetic and copies ran while one was open for 3% -> 14% of each run, Pallas kernels for 0% -> 0%
where the time goes in v1:
time: 186 us
  waiting for transfers between devices  92.7 us (50%)
  starting transfers between devices  28.7 us (15%)
  matrix products  20.8 us (11%)
  blocking collectives  19.5 us (10%)
  between operations  13.7 us (7%)
  local copies, waits for them, and re-layouts  7.57 us (4%)
  other arithmetic  2.75 us (1%)
    all_gather x1, waiting for transfers between devices, shards(): lax.all_gather(out_weight, 'seq', axis=0, tiled=True)  52.6 us
    all_to_all x1, waiting for transfers between devices, shards(): lax.all_to_all(mixed_conv, 'seq', split_axis=1, concat_axis=0, tiled=True)  21.7 us
    all_to_all x1, starting transfers between devices, shards(): lax.all_to_all(product, 'seq', split_axis=0, concat_axis=1, tiled=True)  20.5 us
    all_to_all x1, blocking collectives, shards(): lax.all_to_all(jnp.stack([gated_out] * lax.axis_size('tp')), 'tp', 0, 0)  19.5 us
    all_to_all x1, waiting for transfers between devices, shards(): lax.all_to_all(product, 'seq', split_axis=0, concat_axis=1, tiled=True)  16 us
    dot_general x12, matrix products, right_apply(): return jnp.einsum('ckn,nm->ckm', signal, phase, precision=precise)  9.3 us
    dot_general x1, matrix products, shards(): lax.dot_general(full_rows, lax.all_gather(out_weight, 'seq', axis=0, tile...  5.36 us
    all_to_all x1, starting transfers between devices, shards(): lax.all_to_all(mixed_conv, 'seq', split_axis=1, concat_axis=0, tiled=True)  4.7 us
  transfers between devices with their start and end apart: 4, of which 4 were waited for; matrix products, arithmetic and copies ran while one was open for 14% of the time, Pallas kernels for 0%

profile of v1, /device:TPU:2, one launch (start us, length us, event | category | flops | bytes accessed | tf_op | source)
XLA Modules:
  0.0 185.7 jit_solution(9408293760398823729)
XLA Ops:
  7.3 1.0 slice.94
  8.4 1.0 slice.95
  9.5 1.0 slice.96
  10.9 3.5 %collective-permute-start = (bf16[3,512,2]{2,1,0:T(8,128)(2,1)S(1)}, bf16[3,512,2]{2,1,0:T(8,128)(2,1)S(1)}, u32[]{:S(2)}, u32[]{:S(2)}) collective-permute-start(bf16[3,512,2]{2,1,0:T(8,128)(2,1)S(1)} %copy.25), channel_id=1, source_target_pairs={{0,8},{8,16},{16,24},{24,32},{32,40},{40,48},{48,56},{56,64},{64,7... | collective-permute-start | bytes 18440 | tf_op jit(solution)/shard_map/ppermute | solution.py:13
  14.5 1.1 reshape.87
  16.1 0.9 fusion.180
  17.0 1.1 fusion.58
  18.0 1.1 fusion.61
  19.1 0.8 fusion.4
  19.9 0.8 convolution_add_fusion.1
  21.0 1.8 collective-permute-done
  23.1 1.4 fusion.47
  24.5 20.5 %all-to-all-start = ((bf16[64,8,128]{2,1,0:T(8,128)(2,1)}), bf16[64,8,128]{2,1,0:T(8,128)(2,1)S(1)}, u32[]{:S(2)}, u32[]{:S(2)}) async-start(bf16[64,8,128]{2,1,0:T(8,128)(2,1)} %fusion.47), calls=%async_computation | async-start | bytes 262144 | tf_op jit(solution)/shard_map/all_to_all | solution.py:93
  45.0 0.8 fusion.6
  45.8 0.8 convolution_subtract_fusion.1
  46.6 16.0 %all-to-all-done = bf16[64,8,128]{2,1,0:T(8,128)(2,1)S(1)} async-done(((bf16[64,8,128]{2,1,0:T(8,128)(2,1)}), bf16[64,8,128]{2,1,0:T(8,128)(2,1)S(1)}, u32[]{:S(2)}, u32[]{:S(2)}) %all-to-all-start) | async-done | bytes 131104 | tf_op jit(solution)/shard_map/all_to_all | solution.py:93
  62.7 0.9 convolution_bitcast_fusion
  63.6 0.9 convolution_bitcast_fusion.1
  64.5 0.8 fusion.48
  65.3 0.8 fusion.49
  66.1 0.8 convolution_subtract_fusion.2
  66.9 0.9 multiply_add_fusion
  68.5 0.7 fusion.67
  69.3 0.7 convolution_subtract_fusion
  70.8 1.1 fusion.11
  71.9 1.1 fusion.1
  73.3 1.1 copy.32
  74.4 4.7 %all-to-all-start.1 = ((f32[8,64,128]{2,0,1:T(8,128)}), f32[8,64,128]{2,0,1:T(8,128)S(1)}, u32[]{:S(2)}, u32[]{:S(2)}) async-start(f32[8,64,128]{2,0,1:T(8,128)} %copy.32), calls=%async_computation.1 | async-start | bytes 524288 | tf_op jit(solution)/shard_map/all_to_all | solution.py:95
  79.3 21.7 %all-to-all-done.1 = f32[8,64,128]{2,0,1:T(8,128)S(1)} async-done(((f32[8,64,128]{2,0,1:T(8,128)}), f32[8,64,128]{2,0,1:T(8,128)S(1)}, u32[]{:S(2)}, u32[]{:S(2)}) %all-to-all-start.1) | async-done | bytes 262176 | tf_op jit(solution)/shard_map/all_to_all | solution.py:95
  101.5 19.5 %all_to_all.37 = bf16[8,512,128]{2,1,0:T(8,128)(2,1)S(1)} all-to-all(bf16[8,512,128]{2,1,0:T(8,128)(2,1)S(1)} %stack.27), channel_id=1, replica_groups=mesh['seq'=64,'tp'=8] {'tp'}, dimensions={0} | all-to-all | bytes 2097152 | tf_op jit(solution)/shard_map/all_to_all | solution.py:98
  121.0 52.6 %all-gather.2.cloned.1.call-done = bf16[4096,1024]{1,0:T(8,128)(2,1)} async-done(((bf16[64,1024]{1,0:T(8,128)(2,1)}), bf16[4096,1024]{1,0:T(8,128)(2,1)}) %all-gather.2.cloned.1.call-update) | async-done | bytes 8388624 | tf_op jit(solution)/shard_map/all_gather | solution.py:102
  173.5 5.4 %convolution_convert_fusion = bf16[128,1024]{1,0:T(8,128)(2,1)} fusion(bf16[4096,128]{1,0:T(8,128)(2,1)S(1)} %bitcast.109, bf16[4096,1024]{1,0:T(8,128)(2,1)} %all-gather.2.cloned.1.call-done), kind=kOutput, calls=%fused_computation.8 | convolution fusion | flops 1073872896 | bytes 9699328 | tf_op jit(solution)/shard_map/dot_general | solution.py:100
  (27 shorter events, 4.9 us)
Async XLA Ops:
  6.5 16.3 %copy-start.1 = (bf16[512,128]{1,0:T(8,128)(2,1)S(1)}, bf16[512,128]{1,0:T(8,128)(2,1)}, u32[]{:S(2)}) copy-start(bf16[512,128]{1,0:T(8,128)(2,1)} %param.7) | copy-start | bytes 393220
  6.5 16.3 %copy-start = (bf16[512,128]{1,0:T(8,128)(2,1)S(1)}, bf16[512,128]{1,0:T(8,128)(2,1)}, u32[]{:S(2)}) copy-start(bf16[512,128]{1,0:T(8,128)(2,1)} %param.8) | copy-start | bytes 393220
  6.5 167.0 %all-gather.2.cloned.1.call-start = ((), (), s32[]{:S(2)}) async-start(), calls=%async_computation.3 | async-start | bytes 8519680 | tf_op jit(solution)/shard_map/all_gather | solution.py:102
  10.9 11.8 %collective-permute-start = (bf16[3,512,2]{2,1,0:T(8,128)(2,1)S(1)}, bf16[3,512,2]{2,1,0:T(8,128)(2,1)S(1)}, u32[]{:S(2)}, u32[]{:S(2)}) collective-permute-start(bf16[3,512,2]{2,1,0:T(8,128)(2,1)S(1)} %copy.25), channel_id=1, source_target_pairs={{0,8},{8,16},{16,24},{24,32},{32,40},{40,48},{48,56},{56,64},{64,7... | collective-permute-start | bytes 18440 | tf_op jit(solution)/shard_map/ppermute | solution.py:13
  24.5 38.1 %all-to-all-start = ((bf16[64,8,128]{2,1,0:T(8,128)(2,1)}), bf16[64,8,128]{2,1,0:T(8,128)(2,1)S(1)}, u32[]{:S(2)}, u32[]{:S(2)}) async-start(bf16[64,8,128]{2,1,0:T(8,128)(2,1)} %fusion.47), calls=%async_computation | async-start | bytes 262144 | tf_op jit(solution)/shard_map/all_to_all | solution.py:93
  66.1 13.0 %copy-start.2 = (bf16[512,128]{1,0:T(8,128)(2,1)S(1)}, bf16[512,128]{1,0:T(8,128)(2,1)}, u32[]{:S(2)}) copy-start(bf16[512,128]{1,0:T(8,128)(2,1)} %param.6) | copy-start | bytes 393220
  74.4 26.5 %all-to-all-start.1 = ((f32[8,64,128]{2,0,1:T(8,128)}), f32[8,64,128]{2,0,1:T(8,128)S(1)}, u32[]{:S(2)}, u32[]{:S(2)}) async-start(f32[8,64,128]{2,0,1:T(8,128)} %copy.32), calls=%async_computation.1 | async-start | bytes 524288 | tf_op jit(solution)/shard_map/all_to_all | solution.py:95
Sparse Core Ops, SparseCore 0:
  10.3 163.2 all-gather.1
